TPU v7x, 256 devices: a whole 4x4x8 slice. The times are simulated.
256 devices in a mesh: dp: 2 (over x_lo), expert: 8 (over z), shard: 16 (over x_hi, y, core).
Axes of the slice: x: 4 (x_hi: 2, x_lo: 2; x = x_hi * 2 + x_lo), y: 4, z: 8, core: 2. Of those that a mesh axis runs over, the one named last changes fastest.
Arguments:
- tokens: bfloat16 [2048, 6144], P(('dp', 'expert', 'shard')), may hold values from -6 to 6
- gate_up_weight: bfloat16 [8, 2, 8192, 6144], P(None, None, ('dp', 'expert', 'shard')), may hold values from -0.078125 to 0.078125
- down_weight: bfloat16 [8, 8192, 6144], P(None, ('dp', 'expert', 'shard')), may hold values from -0.0625 to 0.0625
- expert_ids: int32 [2048, 2], P(('dp', 'expert', 'shard')), may hold values from 0 to 7, as said below
- slot_ids: int32 [2048, 2], P(('dp', 'expert', 'shard')), may hold values from 0 to 3, as said below
- gate_values: float32 [2048, 2], P(('dp', 'expert', 'shard')), may hold values from 0.1 to 1
- old_place: int32 [8], replicated, may hold values from 0 to 7, each once
- new_place: int32 [8], replicated, may hold values from 0 to 7, each once
Outputs:
- mixed_out: bfloat16 [2048, 6144], P(('dp', 'expert', 'shard'))
Inputs may be any that keep to these rules, and one draw needn't show every extreme that they name: `expert_ids`: each token names 2 different experts; among the 8 tokens of one block no expert is named more than 4 times, and one expert is named exactly 4 times in every block. `slot_ids`: within one block, two choices that name the same expert have different slots. `old_place`: each expert number appears once. `new_place`: each expert number appears once.
All inputs are finite; a program needn't handle non-finite values.
Results may differ from a plain program's by a relative error of at most 0.02.
Values may be sent and summed in bfloat16 or wider, within the bound.
A program may use at most 128 MiB of HBM per device.

v0:
```python
import jax
import jax.numpy as jnp
from jax import lax
from jax.sharding import PartitionSpec as P


def placement_order(old_place, new_place):
    slot_total = old_place.shape[0]
    matches = (new_place[:, None] == old_place[None, :]).astype(jnp.int32)
    return jnp.sum(matches * jnp.arange(slot_total, dtype=jnp.int32)[None, :], axis=1)


def swiglu_rows(row_block, pair_weight):
    gate_up = jnp.einsum("rd,gud->rgu", row_block, pair_weight, preferred_element_type=jnp.float32)
    return (jax.nn.silu(gate_up[:, 0]) * gate_up[:, 1]).astype(jnp.bfloat16)


def local(
    tokens, gate_up_weight, down_weight, expert_ids, slot_ids, gate_values, old_place, new_place
):
    experts = gate_up_weight.shape[0]
    sliver = gate_up_weight.shape[2]
    model_width = tokens.shape[1]
    tok_rows = tokens.shape[0]
    choices_per_token = expert_ids.shape[1]
    capacity = 2 * tok_rows * choices_per_token // experts
    cell_count = experts * capacity
    data_ways = lax.axis_size("dp")
    slot_order = placement_order(old_place, new_place)
    cell_ids = expert_ids * capacity + slot_ids
    cell_range = jnp.arange(cell_count, dtype=jnp.int32)
    cell_hits = (cell_ids[:, :, None] == cell_range[None, None, :]).astype(jnp.float32)
    token_picks = jnp.sum(cell_hits, axis=1)
    dispatched = jnp.dot(
        token_picks.T.astype(jnp.bfloat16), tokens, preferred_element_type=jnp.float32
    ).astype(jnp.bfloat16)
    received = lax.all_to_all(
        dispatched.reshape(experts, capacity, model_width),
        "expert",
        split_axis=0,
        concat_axis=0,
        tiled=True,
    )
    own_rows = received.reshape(cell_count, model_width)
    sectioned_in = gate_up_weight.reshape(experts, 2, data_ways, sliver // data_ways, model_width)
    sectioned_down = down_weight.reshape(experts, 1, data_ways, sliver // data_ways, model_width)
    sectioned_in = jnp.take(sectioned_in, slot_order, axis=0)
    sectioned_down = jnp.take(sectioned_down, slot_order, axis=0)
    relaid_in, relaid_down = (
        lax.all_to_all(
            lax.all_to_all(sectioned_in, "dp", split_axis=2, concat_axis=3, tiled=True),
            "expert",
            split_axis=0,
            concat_axis=3,
            tiled=True,
        ),
        lax.all_to_all(
            lax.all_to_all(sectioned_down, "dp", split_axis=2, concat_axis=3, tiled=True),
            "expert",
            split_axis=0,
            concat_axis=3,
            tiled=True,
        ),
    )
    full_in, full_down = (
        lax.all_gather(relaid_in, "dp", axis=3, tiled=True),
        lax.all_gather(relaid_down, "dp", axis=3, tiled=True),
    )
    pair_in = full_in.reshape(2, -1, model_width)
    pair_down = full_down.reshape(-1, model_width)
    group_rows = lax.all_gather(own_rows, "shard", axis=0, tiled=True)
    summed = lax.psum_scatter(
        jnp.dot(
            swiglu_rows(group_rows, pair_in), pair_down, preferred_element_type=jnp.float32
        ).astype(jnp.bfloat16),
        "shard",
        scatter_dimension=0,
        tiled=True,
    )
    returned = lax.all_to_all(
        summed.reshape(experts, capacity, model_width),
        "expert",
        split_axis=0,
        concat_axis=0,
        tiled=True,
    )
    combine_weights = jnp.sum(cell_hits * gate_values[:, :, None], axis=1)
    mixed_out = jnp.dot(
        combine_weights,
        returned.reshape(cell_count, model_width).astype(jnp.float32),
        precision=lax.Precision.HIGHEST,
    )
    return mixed_out.astype(jnp.bfloat16)


def solution(mesh):
    in_specs = (
        P(("dp", "expert", "shard"), None),
        P(None, None, ("dp", "expert", "shard"), None),
        P(None, ("dp", "expert", "shard"), None),
        P(("dp", "expert", "shard"), None),
        P(("dp", "expert", "shard"), None),
        P(("dp", "expert", "shard"), None),
        P(),
        P(),
    )
    out_specs = P(("dp", "expert", "shard"), None)
    return jax.shard_map(local, mesh=mesh, in_specs=in_specs, out_specs=out_specs, check_vma=False)
```

profile of v0, /device:TPU:8, one launch (start us, length us, event | category | flops | bytes accessed | tf_op | source)
XLA Modules:
  0.0 681.6 jit_solution(10519561180992360223)
XLA Ops:
  6.5 0.0 copy-start
  6.5 0.8 multiply_add_fusion
  7.4 0.9 convert_reduce_fusion
  8.3 1.2 convolution_convert_fusion.1
  9.5 0.9 reshape.64
  10.4 8.5 %all-to-all-start = ((bf16[8,4,6144]{2,1,0:T(4,128)(2,1)}), bf16[8,4,6144]{2,1,0:T(4,128)(2,1)S(1)}, u32[]{:S(2)}, u32[]{:S(2)}) async-start(bf16[8,4,6144]{2,1,0:T(4,128)(2,1)} %reshape.64), calls=%async_computation | async-start | bytes 786432 | tf_op jit(solution)/shard_map/all_to_all | solution.py:37
  18.8 0.9 select_reduce_fusion.1
  19.7 6.4 gather_fusion
  26.1 3.5 broadcast_select_fusion
  29.6 3.1 copy.24
  32.6 0.9 all-to-all-done
  33.5 6.3 all-to-all-start.1
  39.8 0.0 all-gather.4.cloned.1.call-start
  39.9 0.9 reshape.65
  40.7 0.0 all-gather.4.cloned.1.call-update
  40.8 0.0 all-gather.6.cloned.1.call-start
  40.8 89.5 %all-to-all-done.1 = bf16[8,2,2,16,6144]{4,3,1,0,2:T(8,128)(2,1)} async-done(((bf16[8,2,2,16,6144]{4,3,1,0,2:T(8,128)(2,1)}), bf16[8,2,2,16,6144]{4,3,1,0,2:T(8,128)(2,1)}, u32[]{:S(2)}, u32[]{:S(2)}) %all-to-all-start.1) | async-done | bytes 6291488 | tf_op jit(solution)/shard_map/all_to_all | solution.py:51
  130.3 3.5 copy.25
  133.8 145.8 %all_to_all.64 = bf16[8,2,1,32,6144]{4,3,1,2,0:T(8,128)(2,1)S(1)} all-to-all(bf16[8,2,1,32,6144]{4,3,1,2,0:T(8,128)(2,1)S(1)} %bitcast.37), channel_id=1, replica_groups=mesh['dp'=2,'expert'=8,'shard'=16] {'expert'}, dimensions={0} | all-to-all | bytes 12582912 | tf_op jit(solution)/shard_map/all_to_all | solution.py:50
  279.7 3.1 copy.27
  282.8 0.0 all-gather.6.cloned.1.call-update
  282.8 0.0 all-gather.8.cloned.1.call-start
  282.8 0.0 copy-done
  282.8 2.4 gather_fusion.1
  285.3 2.3 bitcast_select_fusion
  287.5 0.3 copy.28
  287.9 63.1 %all_to_all.65 = bf16[8,1,2,16,6144]{4,3,0,1,2:T(8,128)(2,1)S(1)} all-to-all(bf16[8,1,2,16,6144]{4,3,0,1,2:T(8,128)(2,1)S(1)} %copy.28), channel_id=1, replica_groups=mesh['dp'=2,'expert'=8,'shard'=16] {'dp'}, dimensions={2} | all-to-all | bytes 6291456 | tf_op jit(solution)/shard_map/all_to_all | solution.py:58
  350.9 0.3 copy.29
  351.2 66.1 %all_to_all.66 = bf16[8,1,1,32,6144]{4,3,2,1,0:T(8,128)(2,1)} all-to-all(bf16[8,1,1,32,6144]{4,3,2,1,0:T(8,128)(2,1)S(1)} %bitcast.40), channel_id=1, replica_groups=mesh['dp'=2,'expert'=8,'shard'=16] {'expert'}, dimensions={0} | all-to-all | bytes 6291456 | tf_op jit(solution)/shard_map/all_to_all | solution.py:57
  417.4 0.0 all-gather.8.cloned.1.call-update
  417.4 0.0 reduce-scatter.2.cloned.1.call-start
  417.5 0.0 all-gather.4.cloned.1.call-done
  417.5 41.2 %all-gather.6.cloned.1.call-done = bf16[1,2,1,512,6144]{4,3,1,2,0:T(8,128)(2,1)} async-done(((bf16[1,2,1,256,6144]{4,3,1,2,0:T(8,128)(2,1)}), bf16[1,2,1,512,6144]{4,3,1,2,0:T(8,128)(2,1)}) %all-gather.6.cloned.1.call-update) | async-done | bytes 12582928 | tf_op jit(solution)/shard_map/all_gather | solution.py:66
  458.6 12.5 %fusion = f32[512,2,512]{2,0,1:T(8,128)} fusion(bf16[1,2,1,512,6144]{4,3,1,2,0:T(8,128)(2,1)} %all-gather.6.cloned.1.call-done, bf16[512,6144]{1,0:T(8,128)(2,1)} %all-gather.4.cloned.1.call-done), kind=kOutput, calls=%fused_computation.2 | convolution fusion | flops 6442450944 | bytes 20971520 | tf_op jit(solution)/shard_map/rd,gud->rgu/dot_general | solution.py:14
  471.2 72.6 %all-gather.8.cloned.1.call-done = bf16[1,1,1,512,6144]{4,3,2,1,0:T(8,128)(2,1)} async-done(((bf16[1,1,1,256,6144]{4,3,2,1,0:T(8,128)(2,1)}), bf16[1,1,1,512,6144]{4,3,2,1,0:T(8,128)(2,1)}) %all-gather.8.cloned.1.call-update) | async-done | bytes 6291472 | tf_op jit(solution)/shard_map/all_gather | solution.py:67
  543.8 0.0 copy-start.1
  543.8 9.7 %convolution_convert_fusion = bf16[512,6144]{1,0:T(8,128)(2,1)} fusion(bf16[1,1,1,512,6144]{4,3,2,1,0:T(8,128)(2,1)} %all-gather.8.cloned.1.call-done, f32[512,2,512]{2,0,1:T(8,128)} %fusion), kind=kOutput, calls=%fused_computation.4 | convolution fusion | flops 3225944064 | bytes 14680064 | tf_op jit(solution)/shard_map/dot_general | solution.py:73
  553.5 0.0 reduce-scatter.2.cloned.1.call-update
  553.6 98.3 %reduce-scatter.2.cloned.1.call-done = bf16[32,6144]{1,0:T(8,128)(2,1)} async-done(((bf16[512,6144]{1,0:T(8,128)(2,1)}), bf16[32,6144]{1,0:T(8,128)(2,1)}) %reduce-scatter.2.cloned.1.call-update) | async-done | bytes 393232 | tf_op jit(solution)/shard_map/reduce_scatter | solution.py:72
  651.9 1.1 reshape.70
  653.0 20.0 %all_to_all.67 = bf16[8,4,6144]{2,1,0:T(4,128)(2,1)} all-to-all(bf16[8,4,6144]{2,1,0:T(4,128)(2,1)S(1)} %reshape.70), channel_id=1, replica_groups=mesh['dp'=2,'expert'=8,'shard'=16] {'expert'}, dimensions={0} | all-to-all | bytes 786432 | tf_op jit(solution)/shard_map/all_to_all | solution.py:80
  673.1 1.1 reshape.71
  674.1 0.9 convolution_convert_fusion.2
  675.1 0.0 copy-done.1
  (3 shorter events, 0.0 us)
Async XLA Ops:
  6.5 276.3 %copy-start = (bf16[8,32,6144]{2,1,0:T(8,128)(2,1)S(1)}, bf16[8,32,6144]{2,1,0:T(8,128)(2,1)}, u32[]{:S(2)}) copy-start(bf16[8,32,6144]{2,1,0:T(8,128)(2,1)} %param.10) | copy-start | bytes 9437188
  10.4 23.2 %all-to-all-start = ((bf16[8,4,6144]{2,1,0:T(4,128)(2,1)}), bf16[8,4,6144]{2,1,0:T(4,128)(2,1)S(1)}, u32[]{:S(2)}, u32[]{:S(2)}) async-start(bf16[8,4,6144]{2,1,0:T(4,128)(2,1)} %reshape.64), calls=%async_computation | async-start | bytes 786432 | tf_op jit(solution)/shard_map/all_to_all | solution.py:37
  33.5 96.8 %all-to-all-start.1 = ((bf16[8,2,2,16,6144]{4,3,1,0,2:T(8,128)(2,1)}), bf16[8,2,2,16,6144]{4,3,1,0,2:T(8,128)(2,1)}, u32[]{:S(2)}, u32[]{:S(2)}) async-start(bf16[8,2,2,16,6144]{4,3,1,0,2:T(8,128)(2,1)} %copy.24), calls=%async_computation.1 | async-start | bytes 12582912 | tf_op jit(solution)/shard_map/all_to_all | solution.py:51
  39.8 377.6 %all-gather.4.cloned.1.call-start = ((), (), s32[]{:S(2)}) async-start(), calls=%async_computation.7 | async-start | bytes 6684672 | tf_op jit(solution)/shard_map/all_gather | solution.py:71
  40.8 417.9 %all-gather.6.cloned.1.call-start = ((), (), s32[]{:S(2)}) async-start(), calls=%async_computation.8 | async-start | bytes 18874368 | tf_op jit(solution)/shard_map/all_gather | solution.py:66
  282.8 261.0 %all-gather.8.cloned.1.call-start = ((), (), s32[]{:S(2)}) async-start(), calls=%async_computation.9 | async-start | bytes 9437184 | tf_op jit(solution)/shard_map/all_gather | solution.py:67
  417.4 234.5 %reduce-scatter.2.cloned.1.call-start = ((), (), s32[]{:S(2)}) async-start(), calls=%async_computation.10 | async-start | bytes 6684672 | tf_op jit(solution)/shard_map/reduce_scatter | solution.py:72
  543.8 131.2 %copy-start.1 = (bf16[8,32,6144]{2,1,0:T(8,128)(2,1)S(1)}, bf16[8,32,6144]{2,1,0:T(8,128)(2,1)}, u32[]{:S(2)}) copy-start(bf16[8,32,6144]{2,1,0:T(8,128)(2,1)} %param.10) | copy-start | bytes 9437188
Sparse Core Ops, SparseCore 0:
  43.4 90.1 all-gather.3
  282.9 175.6 all-gather.5
  460.4 83.3 all-gather.7
  553.7 98.1 reduce-scatter.1
where the time goes:
time: 682 us
  waiting for transfers between devices  303 us (44%)
  blocking collectives  295 us (43%)
  matrix products  24.3 us (4%)
  local copies, waits for them, and re-layouts  23.1 us (3%)
  starting transfers between devices  15 us (2%)
  between operations  13.2 us (2%)
  other arithmetic  8.31 us (1%)
    all_to_all x1, blocking collectives, local(): lax.all_to_all(lax.all_to_all(sectioned_in, 'dp', split_axis=2, concat_ax...  146 us
    reduce_scatter x1, waiting for transfers between devices, local(): lax.psum_scatter(jnp.dot(swiglu_rows(group_rows, pair_in), pair_down, pre...  98.3 us
    all_to_all x1, waiting for transfers between devices, local(): lax.all_to_all(sectioned_in, 'dp', split_axis=2, concat_axis=3, tiled=True)  89.5 us
    all_gather x1, waiting for transfers between devices, local(): lax.all_gather(relaid_down, 'dp', axis=3, tiled=True)  72.6 us
    all_to_all x1, blocking collectives, local(): lax.all_to_all(lax.all_to_all(sectioned_down, 'dp', split_axis=2, concat_...  66.1 us
    all_to_all x1, blocking collectives, local(): lax.all_to_all(sectioned_down, 'dp', split_axis=2, concat_axis=3, tiled=T...  63.1 us
    all_gather x1, waiting for transfers between devices, local(): lax.all_gather(relaid_in, 'dp', axis=3, tiled=True)  41.2 us
    all_to_all x1, blocking collectives, local(): lax.all_to_all(summed.reshape(experts, capacity, model_width), 'expert',...  20 us
  transfers between devices with their start and end apart: 6, of which 5 were waited for; matrix products, arithmetic and copies ran while one was open for 6% of the time, Pallas kernels for 0%

commit v1 on v0

--- a/solution.py
+++ b/solution.py
@@ -2,6 +2,20 @@
 import jax.numpy as jnp
 from jax import lax
 from jax.sharding import PartitionSpec as P
+
+
+def _touch_paths(q_in, k_dim, arr):
+    near, prior = (q_in.shape[:k_dim], q_in.shape[k_dim + 1 :])
+    even = q_in.reshape(*near, arr, -1, *prior)
+    return jnp.moveaxis(even, k_dim, 0)
+
+
+def note_the_threads(a0, at_axis):
+    a0 = jnp.moveaxis(a0, 0, at_axis)
+    tile_out = a0.shape
+    return a0.reshape(
+        *tile_out[:at_axis], tile_out[at_axis] * tile_out[at_axis + 1], *tile_out[at_axis + 2 :]
+    )
 
 
 def placement_order(old_place, new_place):
@@ -46,6 +60,22 @@
     sectioned_down = down_weight.reshape(experts, 1, data_ways, sliver // data_ways, model_width)
     sectioned_in = jnp.take(sectioned_in, slot_order, axis=0)
     sectioned_down = jnp.take(sectioned_down, slot_order, axis=0)
+
+    def treat_threads(vals, ax_name, tile_in, local_array):
+        tall = lax.axis_size(ax_name)
+        formed = lax.axis_index(ax_name)
+        h_now, z2 = (tall, formed)
+        then = _touch_paths(vals, tile_in, h_now)
+        dev = 1
+        found = [then[z2]]
+        while dev < h_now:
+            raw_out = then[z2 ^ dev]
+            spare = lax.ppermute(raw_out, ax_name, [(to_i, to_i ^ dev) for to_i in range(h_now)])
+            found.append(spare)
+            dev += 1
+        then = jnp.stack(found, axis=0)[z2 ^ jnp.arange(h_now)]
+        return note_the_threads(then, local_array)
+
     relaid_in, relaid_down = (
         lax.all_to_all(
             lax.all_to_all(sectioned_in, "dp", split_axis=2, concat_axis=3, tiled=True),
@@ -54,12 +84,11 @@
             concat_axis=3,
             tiled=True,
         ),
-        lax.all_to_all(
+        treat_threads(
             lax.all_to_all(sectioned_down, "dp", split_axis=2, concat_axis=3, tiled=True),
             "expert",
-            split_axis=0,
-            concat_axis=3,
-            tiled=True,
+            0,
+            3,
         ),
     )
     full_in, full_down = (

time: 682 us -> 690 us (1.012)
  blocking collectives: 295 us -> 20 us
  waiting for transfers between devices: 303 us -> 558 us
  starting transfers between devices: 15 us -> 33.6 us
  local copies, waits for them, and re-layouts: 23.1 us -> 35.5 us
    all_to_all x3 -> x0, blocking collectives: 275 us -> none  [the longest x1 146 us: local(): lax.all_to_all(lax.all_to_all(sectioned_in, 'dp', split_axis=2, concat_ax...]
    all_to_all x0 -> x2, waiting for transfers between devices: none -> 202 us  [the longest x1 137 us: local(): lax.all_to_all(lax.all_to_all(sectioned_in, 'dp', split_axis=2, concat_ax...]
    ppermute x0 -> x7, waiting for transfers between devices: none -> 63.7 us  [treat_threads(): lax.ppermute(raw_out, ax_name, [(to_i, to_i ^ dev) for to_i in range(h_no...]
    all_to_all x0 -> x2, starting transfers between devices: none -> 10.4 us  [the longest x1 6.4 us: local(): lax.all_to_all(lax.all_to_all(sectioned_in, 'dp', split_axis=2, concat_ax...]
    all_gather x1, waiting for transfers between devices: 41.2 us -> 31.8 us  [local(): lax.all_gather(relaid_in, 'dp', axis=3, tiled=True)]
    ppermute x0 -> x7, starting transfers between devices: none -> 8.14 us  [treat_threads(): lax.ppermute(raw_out, ax_name, [(to_i, to_i ^ dev) for to_i in range(h_no...]
  transfers between devices with their start and end apart: 6 -> 15, of which waited for: 5 -> 12; matrix products, arithmetic and copies ran while one was open for 6% -> 7% of each run, Pallas kernels for 0% -> 0%
where the time goes in v1:
time: 690 us; the launch traced here: 689 us
  waiting for transfers between devices  558 us (81%)
  local copies, waits for them, and re-layouts  35.5 us (5%)
  starting transfers between devices  33.6 us (5%)
  matrix products  21.8 us (3%)
  blocking collectives  20 us (3%)
  between operations  13.4 us (2%)
    all_to_all x1, waiting for transfers between devices, local(): lax.all_to_all(lax.all_to_all(sectioned_in, 'dp', split_axis=2, concat_ax...  137 us
    reduce_scatter x1, waiting for transfers between devices, local(): lax.psum_scatter(jnp.dot(swiglu_rows(group_rows, pair_in), pair_down, pre...  98.4 us
    all_to_all x1, waiting for transfers between devices, local(): lax.all_to_all(sectioned_in, 'dp', split_axis=2, concat_axis=3, tiled=True)  89.6 us
    all_gather x1, waiting for transfers between devices, local(): lax.all_gather(relaid_down, 'dp', axis=3, tiled=True)  71.8 us
    all_to_all x1, waiting for transfers between devices, local(): lax.all_to_all(sectioned_down, 'dp', split_axis=2, concat_axis=3, tiled=T...  64.3 us
    ppermute x7, waiting for transfers between devices, treat_threads(): lax.ppermute(raw_out, ax_name, [(to_i, to_i ^ dev) for to_i in range(h_no...  63.7 us
    all_gather x1, waiting for transfers between devices, local(): lax.all_gather(relaid_in, 'dp', axis=3, tiled=True)  31.8 us
    all_to_all x1, blocking collectives, local(): lax.all_to_all(summed.reshape(experts, capacity, model_width), 'expert',...  20 us
  transfers between devices with their start and end apart: 15, of which 12 were waited for; matrix products, arithmetic and copies ran while one was open for 7% of the time, Pallas kernels for 0%

profile of v1, /device:TPU:8, one launch (start us, length us, event | category | flops | bytes accessed | tf_op | source)
XLA Modules:
  0.0 688.8 jit_solution(6858398019625500374)
XLA Ops:
  6.5 0.8 multiply_add_fusion
  7.4 0.9 convert_reduce_fusion
  8.3 1.2 convolution_convert_fusion.1
  9.5 0.9 reshape.81
  10.4 8.5 %all-to-all-start = ((bf16[8,4,6144]{2,1,0:T(4,128)(2,1)}), bf16[8,4,6144]{2,1,0:T(4,128)(2,1)S(1)}, u32[]{:S(2)}, u32[]{:S(2)}) async-start(bf16[8,4,6144]{2,1,0:T(4,128)(2,1)} %reshape.81), calls=%async_computation | async-start | bytes 786432 | tf_op jit(solution)/shard_map/all_to_all | solution.py:51
  18.9 0.9 select_reduce_fusion.1
  19.7 6.4 gather_fusion
  26.1 3.5 broadcast_select_fusion
  29.6 3.0 copy.23
  32.6 0.9 all-to-all-done
  33.5 6.3 all-to-all-start.1
  39.8 0.0 all-gather.4.cloned.1.call-start
  39.9 0.8 reshape.82
  40.8 89.6 %all-to-all-done.1 = bf16[8,2,2,16,6144]{4,3,1,0,2:T(8,128)(2,1)} async-done(((bf16[8,2,2,16,6144]{4,3,1,0,2:T(8,128)(2,1)}), bf16[8,2,2,16,6144]{4,3,1,0,2:T(8,128)(2,1)}, u32[]{:S(2)}, u32[]{:S(2)}) %all-to-all-start.1) | async-done | bytes 6291488 | tf_op jit(solution)/shard_map/all_to_all | solution.py:81
  130.3 6.4 copy.24
  136.8 6.4 all-to-all-start.2
  143.2 0.0 all-gather.6.cloned.1.call-start
  143.2 2.5 gather_fusion.1
  145.7 137.5 %all-to-all-done.2 = bf16[8,2,1,32,6144]{4,3,1,2,0:T(8,128)(2,1)} async-done(((bf16[8,2,1,32,6144]{4,3,1,2,0:T(8,128)(2,1)}), bf16[8,2,1,32,6144]{4,3,1,2,0:T(8,128)(2,1)}, u32[]{:S(2)}, u32[]{:S(2)}) %all-to-all-start.2) | async-done | bytes 6291488 | tf_op jit(solution)/shard_map/all_to_all | solution.py:80
  283.2 6.1 copy.26
  289.3 1.9 copy-done.2
  291.2 0.4 bitcast_select_fusion
  291.6 2.0 copy.27
  293.6 4.0 all-to-all-start.3
  297.6 0.0 all-gather.8.cloned.1.call-start
  297.7 64.3 %all-to-all-done.3 = bf16[8,1,2,16,6144]{4,3,0,1,2:T(8,128)(2,1)S(1)} async-done(((bf16[8,1,2,16,6144]{4,3,0,1,2:T(8,128)(2,1)}), bf16[8,1,2,16,6144]{4,3,0,1,2:T(8,128)(2,1)S(1)}, u32[]{:S(2)}, u32[]{:S(2)}) %all-to-all-start.3) | async-done | bytes 3145760 | tf_op jit(solution)/shard_map/all_to_all | solution.py:88
  362.0 0.3 copy.28
  362.3 0.2 dynamic-slice_bitcast_fusion
  362.5 0.1 collective-permute-start
  362.7 0.1 collective-permute-start.1
  362.8 4.3 collective-permute-start.2
  367.1 3.6 collective-permute-start.4
  370.7 15.6 %collective-permute-done = bf16[1,1,1,32,6144]{4,3,2,1,0:T(8,128)(2,1)S(1)} collective-permute-done((bf16[1,1,1,32,6144]{4,3,2,1,0:T(8,128)(2,1)S(1)}, bf16[1,1,1,32,6144]{4,3,2,1,0:T(8,128)(2,1)S(1)}, u32[]{:S(2)}, u32[]{:S(2)}) %collective-permute-start) | collective-permute-done | bytes 393248 | tf_op jit(solution)/shard_map/ppermute | solution.py:73
  386.3 24.6 %collective-permute-done.1 = bf16[1,1,1,32,6144]{4,3,2,1,0:T(8,128)(2,1)S(1)} collective-permute-done((bf16[1,1,1,32,6144]{4,3,2,1,0:T(8,128)(2,1)S(1)}, bf16[1,1,1,32,6144]{4,3,2,1,0:T(8,128)(2,1)S(1)}, u32[]{:S(2)}, u32[]{:S(2)}) %collective-permute-start.1) | collective-permute-done | bytes 393248 | tf_op jit(solution)/shard_map/ppermute | solution.py:73
  411.0 9.3 %collective-permute-done.2 = bf16[1,1,1,32,6144]{4,3,2,1,0:T(8,128)(2,1)S(1)} collective-permute-done((bf16[1,1,1,32,6144]{4,3,2,1,0:T(8,128)(2,1)S(1)}, bf16[1,1,1,32,6144]{4,3,2,1,0:T(8,128)(2,1)S(1)}, u32[]{:S(2)}, u32[]{:S(2)}) %collective-permute-start.2) | collective-permute-done | bytes 393248 | tf_op jit(solution)/shard_map/ppermute | solution.py:73
  420.3 6.6 collective-permute-done.3
  427.0 7.6 %collective-permute-done.6 = bf16[1,1,1,32,6144]{4,3,2,1,0:T(8,128)(2,1)S(1)} collective-permute-done((bf16[1,1,1,32,6144]{4,3,2,1,0:T(8,128)(2,1)S(1)}, bf16[1,1,1,32,6144]{4,3,2,1,0:T(8,128)(2,1)S(1)}, u32[]{:S(2)}, u32[]{:S(2)}) %collective-permute-start.6) | collective-permute-done | bytes 393248 | tf_op jit(solution)/shard_map/ppermute | solution.py:73
  434.7 2.4 gather_fusion.2
  437.1 0.2 reduce-scatter.2.cloned.1.call-start
  437.3 31.8 %all-gather.6.cloned.1.call-done = bf16[1,2,1,512,6144]{4,3,1,2,0:T(8,128)(2,1)} async-done(((bf16[1,2,1,256,6144]{4,3,1,2,0:T(8,128)(2,1)}), bf16[1,2,1,512,6144]{4,3,1,2,0:T(8,128)(2,1)}) %all-gather.6.cloned.1.call-update) | async-done | bytes 12582928 | tf_op jit(solution)/shard_map/all_gather | solution.py:95
  469.1 11.6 %fusion = f32[512,2,512]{2,0,1:T(8,128)S(1)} fusion(bf16[1,2,1,512,6144]{4,3,1,2,0:T(8,128)(2,1)} %all-gather.6.cloned.1.call-done, bf16[512,6144]{1,0:T(8,128)(2,1)} %all-gather.4.cloned.1.call-done), kind=kOutput, calls=%fused_computation.3 | convolution fusion | flops 6442450944 | bytes 20971520 | tf_op jit(solution)/shard_map/rd,gud->rgu/dot_general | solution.py:28
  480.7 71.8 %all-gather.8.cloned.1.call-done = bf16[1,1,1,512,6144]{4,3,2,1,0:T(8,128)(2,1)} async-done(((bf16[1,1,1,256,6144]{4,3,2,1,0:T(8,128)(2,1)}), bf16[1,1,1,512,6144]{4,3,2,1,0:T(8,128)(2,1)}) %all-gather.8.cloned.1.call-update) | async-done | bytes 6291472 | tf_op jit(solution)/shard_map/all_gather | solution.py:96
  552.5 8.1 %convolution_convert_fusion = bf16[512,6144]{1,0:T(8,128)(2,1)} fusion(bf16[1,1,1,512,6144]{4,3,2,1,0:T(8,128)(2,1)} %all-gather.8.cloned.1.call-done, f32[512,2,512]{2,0,1:T(8,128)S(1)} %fusion), kind=kOutput, calls=%fused_computation.5 | convolution fusion | flops 3225944064 | bytes 14680064 | tf_op jit(solution)/shard_map/dot_general | solution.py:102
  560.7 98.4 %reduce-scatter.2.cloned.1.call-done = bf16[32,6144]{1,0:T(8,128)(2,1)} async-done(((bf16[512,6144]{1,0:T(8,128)(2,1)}), bf16[32,6144]{1,0:T(8,128)(2,1)}) %reduce-scatter.2.cloned.1.call-update) | async-done | bytes 393232 | tf_op jit(solution)/shard_map/reduce_scatter | solution.py:101
  659.1 1.1 reshape.88
  660.2 20.0 %all_to_all.49 = bf16[8,4,6144]{2,1,0:T(4,128)(2,1)} all-to-all(bf16[8,4,6144]{2,1,0:T(4,128)(2,1)S(1)} %reshape.88), channel_id=1, replica_groups=mesh['dp'=2,'expert'=8,'shard'=16] {'expert'}, dimensions={0} | all-to-all | bytes 786432 | tf_op jit(solution)/shard_map/all_to_all | solution.py:109
  680.2 1.1 reshape.89
  681.3 0.9 convolution_convert_fusion.2
  (27 shorter events, 0.3 us)
Async XLA Ops:
  6.5 136.7 %copy-start = (bf16[8,32,6144]{2,1,0:T(8,128)(2,1)S(1)}, bf16[8,32,6144]{2,1,0:T(8,128)(2,1)}, u32[]{:S(2)}) copy-start(bf16[8,32,6144]{2,1,0:T(8,128)(2,1)} %param.10) | copy-start | bytes 9437188
  10.4 23.1 %all-to-all-start = ((bf16[8,4,6144]{2,1,0:T(4,128)(2,1)}), bf16[8,4,6144]{2,1,0:T(4,128)(2,1)S(1)}, u32[]{:S(2)}, u32[]{:S(2)}) async-start(bf16[8,4,6144]{2,1,0:T(4,128)(2,1)} %reshape.81), calls=%async_computation | async-start | bytes 786432 | tf_op jit(solution)/shard_map/all_to_all | solution.py:51
  33.5 96.8 %all-to-all-start.1 = ((bf16[8,2,2,16,6144]{4,3,1,0,2:T(8,128)(2,1)}), bf16[8,2,2,16,6144]{4,3,1,0,2:T(8,128)(2,1)}, u32[]{:S(2)}, u32[]{:S(2)}) async-start(bf16[8,2,2,16,6144]{4,3,1,0,2:T(8,128)(2,1)} %copy.23), calls=%async_computation.1 | async-start | bytes 12582912 | tf_op jit(solution)/shard_map/all_to_all | solution.py:81
  39.8 397.5 %all-gather.4.cloned.1.call-start = ((), (), s32[]{:S(2)}) async-start(), calls=%async_computation.6 | async-start | bytes 6684672 | tf_op jit(solution)/shard_map/all_gather | solution.py:100
  136.8 146.4 %all-to-all-start.2 = ((bf16[8,2,1,32,6144]{4,3,1,2,0:T(8,128)(2,1)}), bf16[8,2,1,32,6144]{4,3,1,2,0:T(8,128)(2,1)}, u32[]{:S(2)}, u32[]{:S(2)}) async-start(bf16[8,2,1,32,6144]{4,3,1,2,0:T(8,128)(2,1)} %bitcast.66), calls=%async_computation.2 | async-start | bytes 12582912 | tf_op jit(solution)/shard_map/all_to_all | solution.py:80
  143.2 326.0 %all-gather.6.cloned.1.call-start = ((), (), s32[]{:S(2)}) async-start(), calls=%async_computation.7 | async-start | bytes 18874368 | tf_op jit(solution)/shard_map/all_gather | solution.py:95
  289.3 1.9 copy-start.2
  293.6 68.4 %all-to-all-start.3 = ((bf16[8,1,2,16,6144]{4,3,0,1,2:T(8,128)(2,1)}), bf16[8,1,2,16,6144]{4,3,0,1,2:T(8,128)(2,1)S(1)}, u32[]{:S(2)}, u32[]{:S(2)}) async-start(bf16[8,1,2,16,6144]{4,3,0,1,2:T(8,128)(2,1)} %copy.27), calls=%async_computation.3 | async-start | bytes 6291456 | tf_op jit(solution)/shard_map/all_to_all | solution.py:88
  297.6 254.9 %all-gather.8.cloned.1.call-start = ((), (), s32[]{:S(2)}) async-start(), calls=%async_computation.8 | async-start | bytes 9437184 | tf_op jit(solution)/shard_map/all_gather | solution.py:96
  362.5 23.7 %collective-permute-start = (bf16[1,1,1,32,6144]{4,3,2,1,0:T(8,128)(2,1)S(1)}, bf16[1,1,1,32,6144]{4,3,2,1,0:T(8,128)(2,1)S(1)}, u32[]{:S(2)}, u32[]{:S(2)}) collective-permute-start(bf16[1,1,1,32,6144]{4,3,2,1,0:T(8,128)(2,1)S(1)} %get-tuple-element.13), channel_id=1, source_target_pairs={{0,16},{16,0},{32,48},{48,32},{64,80},{80,64},{96,112},{112,96},{1... | collective-permute-start | bytes 1179656 | tf_op jit(solution)/shard_map/ppermute | solution.py:73
  362.7 48.2 %collective-permute-start.1 = (bf16[1,1,1,32,6144]{4,3,2,1,0:T(8,128)(2,1)S(1)}, bf16[1,1,1,32,6144]{4,3,2,1,0:T(8,128)(2,1)S(1)}, u32[]{:S(2)}, u32[]{:S(2)}) collective-permute-start(bf16[1,1,1,32,6144]{4,3,2,1,0:T(8,128)(2,1)S(1)} %get-tuple-element.12), channel_id=1, source_target_pairs={{0,32},{16,48},{32,0},{48,16},{64,96},{80,112},{96,64},{112,80},{1... | collective-permute-start | bytes 1179656 | tf_op jit(solution)/shard_map/ppermute | solution.py:73
  362.8 57.5 %collective-permute-start.2 = (bf16[1,1,1,32,6144]{4,3,2,1,0:T(8,128)(2,1)S(1)}, bf16[1,1,1,32,6144]{4,3,2,1,0:T(8,128)(2,1)S(1)}, u32[]{:S(2)}, u32[]{:S(2)}) collective-permute-start(bf16[1,1,1,32,6144]{4,3,2,1,0:T(8,128)(2,1)S(1)} %get-tuple-element.11), channel_id=1, source_target_pairs={{0,48},{16,32},{32,16},{48,0},{64,112},{80,96},{96,80},{112,64},{1... | collective-permute-start | bytes 1179656 | tf_op jit(solution)/shard_map/ppermute | solution.py:73
  367.1 59.8 %collective-permute-start.3 = (bf16[1,1,1,32,6144]{4,3,2,1,0:T(8,128)(2,1)S(1)}, bf16[1,1,1,32,6144]{4,3,2,1,0:T(8,128)(2,1)S(1)}, u32[]{:S(2)}, u32[]{:S(2)}) collective-permute-start(bf16[1,1,1,32,6144]{4,3,2,1,0:T(8,128)(2,1)S(1)} %get-tuple-element.10), channel_id=1, source_target_pairs={{0,64},{16,80},{32,96},{48,112},{64,0},{80,16},{96,32},{112,48},{1... | collective-permute-start | bytes 1179656 | tf_op jit(solution)/shard_map/ppermute | solution.py:73
  367.1 59.8 %collective-permute-start.4 = (bf16[1,1,1,32,6144]{4,3,2,1,0:T(8,128)(2,1)S(1)}, bf16[1,1,1,32,6144]{4,3,2,1,0:T(8,128)(2,1)S(1)}, u32[]{:S(2)}, u32[]{:S(2)}) collective-permute-start(bf16[1,1,1,32,6144]{4,3,2,1,0:T(8,128)(2,1)S(1)} %get-tuple-element.9), channel_id=1, source_target_pairs={{0,80},{16,64},{32,112},{48,96},{64,16},{80,0},{96,48},{112,32},{1... | collective-permute-start | bytes 1179656 | tf_op jit(solution)/shard_map/ppermute | solution.py:73
  386.3 40.7 %collective-permute-start.5 = (bf16[1,1,1,32,6144]{4,3,2,1,0:T(8,128)(2,1)S(1)}, bf16[1,1,1,32,6144]{4,3,2,1,0:T(8,128)(2,1)S(1)}, u32[]{:S(2)}, u32[]{:S(2)}) collective-permute-start(bf16[1,1,1,32,6144]{4,3,2,1,0:T(8,128)(2,1)S(1)} %get-tuple-element.8), channel_id=1, source_target_pairs={{0,96},{16,112},{32,64},{48,80},{64,32},{80,48},{96,0},{112,16},{1... | collective-permute-start | bytes 1179656 | tf_op jit(solution)/shard_map/ppermute | solution.py:73
  410.9 23.7 %collective-permute-start.6 = (bf16[1,1,1,32,6144]{4,3,2,1,0:T(8,128)(2,1)S(1)}, bf16[1,1,1,32,6144]{4,3,2,1,0:T(8,128)(2,1)S(1)}, u32[]{:S(2)}, u32[]{:S(2)}) collective-permute-start(bf16[1,1,1,32,6144]{4,3,2,1,0:T(8,128)(2,1)S(1)} %get-tuple-element.7), channel_id=1, source_target_pairs={{0,112},{16,96},{32,80},{48,64},{64,48},{80,32},{96,16},{112,0},{1... | collective-permute-start | bytes 1179656 | tf_op jit(solution)/shard_map/ppermute | solution.py:73
  437.1 222.0 %reduce-scatter.2.cloned.1.call-start = ((), (), s32[]{:S(2)}) async-start(), calls=%async_computation.9 | async-start | bytes 6684672 | tf_op jit(solution)/shard_map/reduce_scatter | solution.py:101
  560.7 121.6 %copy-start.1 = (bf16[8,32,6144]{2,1,0:T(8,128)(2,1)S(1)}, bf16[8,32,6144]{2,1,0:T(8,128)(2,1)}, u32[]{:S(2)}) copy-start(bf16[8,32,6144]{2,1,0:T(8,128)(2,1)} %param.10) | copy-start | bytes 9437188
Sparse Core Ops, SparseCore 0:
  43.4 90.1 all-gather.3
  289.4 179.6 all-gather.5
  470.9 81.5 all-gather.7
  560.8 98.1 reduce-scatter.1
